TPU v7x, 32 devices: a whole 2x2x4 slice. The times are simulated.
32 devices in a mesh: dom: 8 (over y, x, core), sub: 4 (over z).
Axes of the slice: x: 2, y: 2, z: 4, core: 2. Of those that a mesh axis runs over, the one named last changes fastest.
Arguments:
- dofs: float32 [56, 9, 4096], P(None, None, ('dom', 'sub')), may hold values from -6 to 6
- star: float32 [3, 9, 9, 4096], P(None, None, None, ('dom', 'sub')), may hold values from -2 to 2
- flux_own: float32 [4, 9, 9, 4096], P(None, None, None, ('dom', 'sub')), may hold values from -2 to 2
- flux_nbr: float32 [4, 9, 9, 4096], P(None, None, None, ('dom', 'sub')), may hold values from -2 to 2
- cohesion: float32 [4096], P(('dom', 'sub')), may hold values from 0.5 to 8
- cluster: int32 [4096], P(('dom', 'sub')), may hold values from 0 to 1, as said below
- face_source: int32 [4, 4096], P(None, ('dom', 'sub')), may hold values from 0 to 607, as said below
- orient: int32 [4, 4096], P(None, ('dom', 'sub')), may hold values from 0 to 2
- send_rows: int32 [8, 4, 3, 4, 8], P('dom', 'sub'), may hold values from 0 to 511
- stiffness: float32 [3, 56, 56], replicated, may hold values from -0.75 to 0.75
- project: float32 [4, 21, 56], replicated, may hold values from -0.75 to 0.75
- lift: float32 [4, 56, 21], replicated, may hold values from -0.625 to 0.625
- rotate: float32 [3, 21, 21], replicated, may hold values from -1.25 to 1.25
Outputs:
- evolved: float32 [56, 9, 4096], P(None, None, ('dom', 'sub'))
Inputs may be any that keep to these rules, and one draw needn't show every extreme that they name: 0 marks an element of the fine cluster (two steps of 0.5), 1 one of the coarse cluster (one step of 1). The share of fine elements differs from device to device. `face_source`: values below 512 name one of the device's own faces (face times 128 plus element); the value 4 * 128 + q names received row q, q = (direction * 4 + sender sub index) * 8 + slot. Of the 8 slots of every sender the last 1 to 8 are named, each by exactly one face of the device, and all 8 for at least one sender of every device.
All inputs are finite; a program needn't handle non-finite values.
Results may differ from a plain program's by a relative error of at most 0.0003.
Values sent between devices are 32-bit elements; how exact they have to be, the bound alone decides.
A program may use at most 64 MiB of HBM per device.

v0:
```python
import functools
import math

import jax
import jax.numpy as jnp
from jax import lax
from jax.experimental import pallas as pl
from jax.experimental.pallas import tpu as pltpu
from jax.sharding import PartitionSpec as P

ORDER = 6
step_time = 0.5
relax_time = 0.5
f32 = jnp.float32
bf16 = jnp.bfloat16
MESH = pl.DeviceIdType.MESH


def series_weights():
    first, second = [], []
    for k in range(ORDER):
        sign = (-1.0) ** k / math.factorial(k + 1)
        low, high = step_time ** (k + 1), (2.0 * step_time) ** (k + 1)
        first.append(sign * low)
        second.append(sign * (high - low))
    return first + second


def round_up(n, m):
    return -(-n // m) * m


def parts(x):
    high = x.astype(bf16).astype(f32)
    return high, x - high


def split_rows(x):
    high = x.astype(bf16)
    return high, (x - high.astype(f32)).astype(bf16)


def kernel(dims, *refs):
    count = 13
    loaded = refs[count + 1 : 2 * count + 1]
    body(dims, refs[:count], loaded, refs[-1], *loaded, refs[count], *refs[2 * count + 1 : -1])


def body(
    dims,
    given,
    loaded,
    load_sem,
    dofs,
    star,
    flux_own,
    flux_nbr,
    cohesion,
    cluster,
    face_source,
    orient,
    send_rows,
    stiff,
    project,
    lift,
    rotate,
    out,
    mats,
    lift_t,
    rot_s,
    send_s,
    a_mat,
    l_mat,
    r_ref,
    cat,
    prod,
    u0,
    u1,
    acc1,
    acc2,
    upd,
    tr,
    tcat,
    oh,
    pick,
    nb,
    terms,
    tcat3,
    send,
    recv,
    send_sem,
    recv_sem,
):
    nb_, nq, ne, nf, nsub, ndom, bp, gp, npd = dims
    rows = 3 * nb_
    nrecv = 3 * nsub * 8
    dom, sub = lax.axis_index("dom"), lax.axis_index("sub")

    def peer(direction, k):
        return (
            lax.rem(dom + direction - 1 + ndom, ndom),
            lax.rem(sub + k, nsub),
        )

    links = [(d, k) for d in range(3) for k in range(nsub) if not (d == 1 and k == 0)]
    barrier = pltpu.get_barrier_semaphore()
    for d, k in links:
        pl.semaphore_signal(barrier, inc=1, device_id=peer(d, k), device_id_type=MESH)

    loads = [
        pltpu.make_async_copy(source, place, load_sem.at[n])
        for n, (source, place) in enumerate(zip(given, loaded))
    ]
    early = (0, 1, 8, 9, 10)
    for n in list(early) + [n for n in range(len(loads)) if n not in early]:
        loads[n].start()

    def lanes(q):
        return slice(q * ne, (q + 1) * ne)

    pad_rows = jnp.zeros((bp - nb_, ne), f32)

    def put_cat(q, x):
        high, low = split_rows(jnp.concatenate([x, pad_rows], axis=0))
        cat[0:bp, lanes(q)] = high
        cat[bp : 2 * bp, lanes(q)] = high
        cat[2 * bp : 3 * bp, lanes(q)] = low

    def star_mul(emit):
        for q0 in range(0, nq, 3):
            qs = range(q0, min(q0 + 3, nq))
            accs = [None] * len(qs)
            for d in range(3):
                for p in range(nq):
                    block = prod[d * nb_ : (d + 1) * nb_, lanes(p)]
                    for n, q in enumerate(qs):
                        term = block * star[p, q, d : d + 1, :]
                        accs[n] = term if accs[n] is None else accs[n] + term
            for n, q in enumerate(qs):
                emit(q, accs[n])

    wts = series_weights()

    def pick_weight(k, base):
        value = jnp.float32(wts[base + ORDER - 1])
        for n in range(1, ORDER - 1):
            value = jnp.where(k == n, jnp.float32(wts[base + n]), value)
        return value

    def mat_cat(low, high):
        return jnp.dot(a_mat[low:high, :], cat[...], preferred_element_type=f32)

    def series(second_too):
        def body(k, carry):
            prod[...] = mat_cat(0, rows)
            w1, w2 = pick_weight(k, 0), pick_weight(k, ORDER)

            def emit(q, x):
                put_cat(q, x)
                acc1[:, lanes(q)] = acc1[:, lanes(q)] + w1 * x
                if second_too:
                    acc2[:, lanes(q)] = acc2[:, lanes(q)] + w2 * x

            star_mul(emit)
            return carry

        lax.fori_loop(1, ORDER, body, 0)

    def exchange(phase):
        copies = []
        for d, k in links:
            target = peer(d, k)
            copies.append(
                pltpu.make_async_remote_copy(
                    src_ref=send.at[phase, d * nsub + target[1]],
                    dst_ref=recv.at[phase, (2 - d) * nsub + sub],
                    send_sem=send_sem.at[phase, d * nsub + k],
                    recv_sem=recv_sem.at[phase, (2 - d) * nsub + k],
                    device_id=target,
                    device_id_type=MESH,
                )
            )
        return copies

    def traces(phase):
        for q in range(nq):
            put_cat(q, acc1[:, lanes(q)])
        tr[...] = mat_cat(2 * rows, 2 * rows + nf * gp)
        for f in range(nf):
            own = [tr[f * gp : (f + 1) * gp, lanes(q)] for q in range(nq)]
            own.append(jnp.zeros((npd - nq * gp, ne), f32))
            high, low = split_rows(jnp.concatenate(own, axis=0))
            tcat[0:npd, lanes(f)] = high
            tcat[npd : 2 * npd, lanes(f)] = low
        spots = lax.broadcasted_iota(jnp.int32, (8, nf * ne), 1).astype(f32)
        columns = send_s[...].T
        chosen = jnp.concatenate(
            [
                jnp.where(spots == columns[:, c : c + 1], 1.0, 0.0)
                for c in range(3 * nsub)
            ],
            axis=0,
        ).astype(bf16)
        nt = (((1,), (1,)), ((), ()))
        outgoing = lax.dot_general(
            chosen, tcat[0:npd, :], nt, preferred_element_type=f32
        ) + lax.dot_general(chosen, tcat[npd : 2 * npd, :], nt, preferred_element_type=f32)
        send[phase] = outgoing.reshape(3 * nsub, 8, npd)
        if phase == 0:
            pl.semaphore_wait(barrier, len(links))
        copies = exchange(phase)
        for copy in copies:
            copy.start()
        return copies

    def volume(emit):
        prod[...] = mat_cat(rows, 2 * rows)
        star_mul(emit)

    def flux(source, matrix, first):
        for f in range(nf):
            at = slice(f * gp, (f + 1) * gp)
            if first:
                accs = [None] * nq
            else:
                accs = [terms[at, lanes(q)] for q in range(nq)]
            for p in range(nq):
                block = source[at, lanes(p)]
                for q in range(nq):
                    term = block * matrix[p, q, f : f + 1, :]
                    accs[q] = term if accs[q] is None else accs[q] + term
            for q in range(nq):
                terms[at, lanes(q)] = accs[q]

    def own_side():
        pick[...] = jnp.dot(tcat[...], oh[0 : nf * ne, :], preferred_element_type=f32)
        flux(tr, flux_own, True)

    def other_side(phase, copies):
        for copy in copies:
            copy.wait()
        recv[phase, pl.ds(nsub + sub, 1)] = send[phase, pl.ds(nsub + sub, 1)]
        arrived = recv[phase].reshape(nrecv, npd).T
        high, low = split_rows(arrived)
        far = oh[nf * ne : nf * ne + nrecv, :]
        pick[0:npd, :] = pick[0:npd, :] + jnp.dot(high, far, preferred_element_type=f32)
        pick[npd : 2 * npd, :] = pick[npd : 2 * npd, :] + jnp.dot(
            low, far, preferred_element_type=f32
        )
        r_mat = r_ref[...]
        extra = jnp.zeros((r_mat.shape[1] - 3 * gp, nf * ne), f32)
        for q in range(nq):
            high = pick[q * gp : (q + 1) * gp, :]
            low = pick[npd + q * gp : npd + (q + 1) * gp, :]
            stacked = jnp.concatenate([high, high, low, extra], axis=0).astype(bf16)
            turned = jnp.dot(r_mat, stacked, preferred_element_type=f32)
            for f in range(nf):
                code = jnp.broadcast_to(orient[f : f + 1, :], (gp, ne))
                part = turned[:, lanes(f)]
                nb[f * gp : (f + 1) * gp, lanes(q)] = jnp.where(
                    code == 0,
                    part[0:gp],
                    jnp.where(code == 1, part[gp : 2 * gp], part[2 * gp : 3 * gp]),
                )
        flux(nb, flux_nbr, False)
        high, low = split_rows(terms[...])
        ng = nf * gp
        tcat3[0:ng, :] = high
        tcat3[ng : 2 * ng, :] = high
        tcat3[2 * ng : 3 * ng, :] = low
        return jnp.dot(l_mat[...], tcat3[...], preferred_element_type=f32)

    def plastic(field, relax, emit):
        s = [field[q][0:1, :] for q in range(6)]
        pressure = (s[0] + s[1] + s[2]) / 3.0
        dx, dy, dz = s[0] - pressure, s[1] - pressure, s[2] - pressure
        inv = (
            0.5 * (dx * dx + dy * dy + dz * dz) + s[3] * s[3] + s[4] * s[4] + s[5] * s[5]
        )
        coh = cohesion[...]
        factor = 1.0 - (1.0 - coh / jnp.maximum(jnp.sqrt(inv), coh)) * relax
        mean = (field[0] + field[1] + field[2]) * (1.0 / 3.0)
        for q in range(3):
            emit(q, mean + factor * (field[q] - mean))
        for q in range(3, 6):
            emit(q, factor * field[q])
        for q in range(6, nq):
            emit(q, field[q])

    fine_relax = 1.0 - math.exp(-step_time / relax_time)
    coarse_relax = 1.0 - math.exp(-2.0 * step_time / relax_time)

    mats[...] = jnp.zeros_like(mats)
    for n in early:
        loads[n].wait()
    ng = project.shape[0]
    for d in range(3):
        mats[d * nb_ : (d + 1) * nb_, 0:nb_] = stiff[d]
        mats[rows + d * nb_ : rows + (d + 1) * nb_, 0:nb_] = stiff[d].T
    for f in range(nf):
        at = 2 * rows + f * gp
        mats[at : at + ng, 0:nb_] = project[:, f, :]
    high, low = parts(mats[...])
    a_mat[...] = jnp.concatenate([high, low, high], axis=1).astype(bf16)
    for d in range(3):
        send_s[d * nsub : (d + 1) * nsub, :] = send_rows[d].astype(f32)

    def later_constants():
        lift_t[...] = jnp.zeros_like(lift_t)
        for f in range(nf):
            lift_t[f * gp : f * gp + ng, :] = lift[:, f, :]
        high, low = parts(lift_t[...])
        l_mat[...] = jnp.concatenate([high, low, high], axis=0).T.astype(bf16)
        rot_s[...] = jnp.zeros_like(rot_s)
        for h in range(3):
            rot_s[h * gp : h * gp + ng, 0:ng] = rotate[h]
        high, low = parts(rot_s[...].T)
        blank = jnp.zeros((r_ref.shape[1] - 3 * gp, 3 * gp), f32)
        r_ref[...] = jnp.concatenate([high, low, high, blank], axis=0).T.astype(bf16)

    for q in range(nq):
        x = dofs[q]
        u0[:, lanes(q)] = x
        put_cat(q, x)
        acc1[:, lanes(q)] = wts[0] * x
        acc2[:, lanes(q)] = wts[ORDER] * x
    series(True)
    copies = traces(0)
    for n in range(len(loads)):
        if n not in early:
            loads[n].wait()
    later_constants()
    for f in range(nf):
        code = face_source[f : f + 1, :]
        for r in range(0, nf * ne + nrecv, 32):
            row = lax.broadcasted_iota(jnp.int32, (32, ne), 0) + r
            oh[r : r + 32, lanes(f)] = jnp.where(row == code, 1.0, 0.0).astype(bf16)

    def keep(q, x):
        upd[:, lanes(q)] = x

    volume(keep)
    own_side()
    lifted = other_side(0, copies)
    upd[...] = upd[...] - lifted

    def keep_stepped(q, x):
        u1[:, lanes(q)] = x
        put_cat(q, x)
        acc1[:, lanes(q)] = wts[0] * x

    plastic([u0[:, lanes(q)] + upd[:, lanes(q)] for q in range(nq)], fine_relax, keep_stepped)

    series(False)
    fine = cluster[...] == 0
    for q in range(nq):
        acc1[:, lanes(q)] = jnp.where(fine, acc1[:, lanes(q)], acc2[:, lanes(q)])
    copies = traces(1)

    def keep_second(q, x):
        at = lanes(q)
        u1[:, at] = x + jnp.where(fine, u1[:, at], u0[:, at] + upd[:, at])

    volume(keep_second)
    own_side()
    upd[...] = other_side(1, copies)

    def write(q, x):
        out[q] = x

    plastic(
        [u1[:, lanes(q)] - upd[:, lanes(q)] for q in range(nq)],
        jnp.where(fine, fine_relax, coarse_relax),
        write,
    )


def local(
    mesh,
    dofs,
    star,
    flux_own,
    flux_nbr,
    cohesion,
    cluster,
    face_source,
    orient,
    send_rows,
    stiffness,
    project,
    lift,
    rotate,
):
    nbas, nq, ne = dofs.shape
    nf, ng = project.shape[0], project.shape[1]
    nsub, ndom = mesh.shape["sub"], mesh.shape["dom"]
    bp = round_up(nbas, 16)
    gp = round_up(ng, 8)
    npd = round_up(nq * gp, 32)
    rp = round_up(3 * gp, 16)
    nrecv = 3 * nsub * 8
    dims = (nbas, nq, ne, nf, nsub, ndom, bp, gp, npd)
    vmem = pl.BlockSpec(memory_space=pltpu.VMEM)
    wide = nq * ne
    args = (
        jnp.transpose(dofs, (1, 0, 2)),
        jnp.transpose(star, (1, 2, 0, 3)),
        jnp.transpose(flux_own, (1, 2, 0, 3)),
        jnp.transpose(flux_nbr, (1, 2, 0, 3)),
        cohesion.reshape(1, ne),
        cluster.reshape(1, ne),
        face_source,
        orient,
        send_rows.reshape(send_rows.shape[2:]),
        stiffness,
        jnp.transpose(project, (1, 0, 2)),
        jnp.transpose(lift, (2, 0, 1)),
        rotate,
    )
    result = pl.pallas_call(
        functools.partial(kernel, dims),
        out_shape=jax.ShapeDtypeStruct((nq, nbas, ne), f32),
        in_specs=[pl.BlockSpec(memory_space=pltpu.HBM)] * len(args),
        out_specs=vmem,
        scratch_shapes=[pltpu.VMEM(x.shape, x.dtype) for x in args]
        + [
            pltpu.VMEM((6 * nbas + nf * gp, bp), f32),
            pltpu.VMEM((nf * gp, nbas), f32),
            pltpu.VMEM((3 * gp, gp), f32),
            pltpu.VMEM((3 * nsub, 8), f32),
            pltpu.VMEM((6 * nbas + nf * gp, 3 * bp), bf16),
            pltpu.VMEM((nbas, 3 * nf * gp), bf16),
            pltpu.VMEM((3 * gp, rp), bf16),
            pltpu.VMEM((3 * bp, wide), bf16),
            pltpu.VMEM((3 * nbas, wide), f32),
            pltpu.VMEM((nbas, wide), f32),
            pltpu.VMEM((nbas, wide), f32),
            pltpu.VMEM((nbas, wide), f32),
            pltpu.VMEM((nbas, wide), f32),
            pltpu.VMEM((nbas, wide), f32),
            pltpu.VMEM((nf * gp, wide), f32),
            pltpu.VMEM((2 * npd, nf * ne), bf16),
            pltpu.VMEM((nf * ne + nrecv, nf * ne), bf16),
            pltpu.VMEM((2 * npd, nf * ne), f32),
            pltpu.VMEM((nf * gp, wide), f32),
            pltpu.VMEM((nf * gp, wide), f32),
            pltpu.VMEM((3 * nf * gp, wide), bf16),
            pltpu.VMEM((2, 3 * nsub, 8, npd), f32),
            pltpu.VMEM((2, 3 * nsub, 8, npd), f32),
            pltpu.SemaphoreType.DMA((2, 3 * nsub)),
            pltpu.SemaphoreType.DMA((2, 3 * nsub)),
            pltpu.SemaphoreType.DMA((len(args),)),
        ],
        compiler_params=pltpu.CompilerParams(
            collective_id=0, has_side_effects=True, vmem_limit_bytes=60 * 1024 * 1024
        ),
        name="window",
    )(*args)
    return jnp.transpose(result, (1, 0, 2))


def solution(mesh):
    both = ("dom", "sub")
    placed = (
        P(None, None, both),
        P(None, None, None, both),
        P(None, None, None, both),
        P(None, None, None, both),
        P(both),
        P(both),
        P(None, both),
        P(None, both),
        P("dom", "sub", None, None, None),
        P(),
        P(),
        P(),
        P(),
    )
    return jax.shard_map(
        functools.partial(local, mesh),
        mesh=mesh,
        in_specs=placed,
        out_specs=P(None, None, both),
        check_vma=False,
    )
```

profile of v0, /device:TPU:0, one launch (start us, length us, event | category | flops | bytes accessed | tf_op | source)
XLA Modules:
  0.0 27.7 jit_solution(6595343490927318143)
XLA Ops:
  0.0 26.0 %window.1 = f32[9,56,128]{2,1,0:T(8,128)} custom-call(f32[9,56,128]{2,1,0:T(8,128)} %bitcast.11, f32[9,9,3,128]{3,2,1,0:T(4,128)} %bitcast.12, f32[9,9,4,128]{3,2,1,0:T(4,128)} %bitcast.13, f32[9,9,4,128]{3,2,1,0:T(4,128)} %bitcast.14, f32[1,128]{1,0:T(1,128)} %bitcast.18, s32[1,128]{1,0:T(1,128)} %bitcast.19, s32[4,128]{1,0:T(4,128)} %refs_6_.1, ...), custom_call_target="tpu_custom_call" | custom-call | tf_op jit(solution)/shard_map/window/pallas_call | solution.py:420
  26.0 1.7 %copy.15 = f32[56,9,128]{2,0,1:T(8,128)} copy(f32[56,9,128]{2,0,1:T(8,128)} %bitcast.10) | data formatting | bytes 516096
where the time goes:
time: 27.8 us; the launch traced here: 27.7 us
  Pallas kernels  26 us (94%)
  local copies, waits for them, and re-layouts  1.66 us (6%)
    pallas_call x1, Pallas kernels, local(): pl.pallas_call(functools.partial(kernel, dims), out_shape=jax.ShapeDtypeS...  26 us
    unnamed x1, local copies, waits for them, and re-layouts  1.66 us

commit v1 on v0

--- a/solution.py
+++ b/solution.py
@@ -103,6 +103,14 @@
         )
 
     links = [(d, k) for d in range(3) for k in range(nsub) if not (d == 1 and k == 0)]
+    low = 1 - (2 * sub) // nsub
+    far_first = []
+    for r in range(nsub):
+        place = low * (nsub - 1 - 2 * r) + r
+        apart = lax.rem(place - sub + nsub, nsub)
+        far_first += [(0, apart), (2, apart)]
+        if r + 1 < nsub:
+            far_first.append((1, low * (nsub - 2 * (r + 1)) + r + 1))
     barrier = pltpu.get_barrier_semaphore()
     for d, k in links:
         pl.semaphore_signal(barrier, inc=1, device_id=peer(d, k), device_id_type=MESH)
@@ -168,7 +176,7 @@
 
     def exchange(phase):
         copies = []
-        for d, k in links:
+        for d, k in far_first:
             target = peer(d, k)
             copies.append(
                 pltpu.make_async_remote_copy(
@@ -419,7 +427,7 @@
     )
     result = pl.pallas_call(
         functools.partial(kernel, dims),
-        out_shape=jax.ShapeDtypeStruct((nq, nbas, ne), f32),
+        out_shape=pltpu.VMEM((nq, nbas, ne), f32),
         in_specs=[pl.BlockSpec(memory_space=pltpu.HBM)] * len(args),
         out_specs=vmem,
         scratch_shapes=[pltpu.VMEM(x.shape, x.dtype) for x in args]
@@ -452,10 +460,10 @@
             pltpu.SemaphoreType.DMA((len(args),)),
         ],
         compiler_params=pltpu.CompilerParams(
-            collective_id=0, has_side_effects=True, vmem_limit_bytes=60 * 1024 * 1024
+            collective_id=0, has_side_effects=True, vmem_limit_bytes=48 * 1024 * 1024
         ),
         name="window",
-    )(*args)
+    )(*(pltpu.with_memory_space_constraint(x, pltpu.HBM) for x in args))
     return jnp.transpose(result, (1, 0, 2))
 
 

time: 27.8 us -> 26 us (0.935)
  local copies, waits for them, and re-layouts: 1.66 us -> 0.7 us
  Pallas kernels: 26 us -> 25.1 us
    unnamed x1, local copies, waits for them, and re-layouts: 1.66 us -> 0.7 us
    pallas_call x1, Pallas kernels: 26 us -> 25.1 us  [local(): pl.pallas_call(functools.partial(kernel, dims), out_shape=pltpu.VMEM((nq,...]
where the time goes in v1:
time: 26 us; the launch traced here: 25.8 us
  Pallas kernels  25.1 us (97%)
  local copies, waits for them, and re-layouts  0.7 us (3%)
    pallas_call x1, Pallas kernels, local(): pl.pallas_call(functools.partial(kernel, dims), out_shape=pltpu.VMEM((nq,...  25.1 us
    unnamed x1, local copies, waits for them, and re-layouts  0.7 us

profile of v1, /device:TPU:0, one launch (start us, length us, event | category | flops | bytes accessed | tf_op | source)
XLA Modules:
  0.0 25.8 jit_solution(2829276019238521394)
XLA Ops:
  0.0 25.1 %window.1 = f32[9,56,128]{2,1,0:T(8,128)S(1)} custom-call(f32[9,56,128]{2,1,0:T(8,128)} %bitcast.11, f32[9,9,3,128]{3,2,1,0:T(4,128)} %bitcast.12, f32[9,9,4,128]{3,2,1,0:T(4,128)} %bitcast.13, f32[9,9,4,128]{3,2,1,0:T(4,128)} %bitcast.14, f32[1,128]{1,0:T(1,128)} %bitcast.18, s32[1,128]{1,0:T(1,128)} %bitcast.19, s32[4,128]{1,0:T(4,128)} %refs_6_.1, ...), custom_call_target="tpu_custom_call" | custom-call | tf_op jit(solution)/shard_map/window/pallas_call | solution.py:428
  25.1 0.7 %copy.15 = f32[56,9,128]{2,0,1:T(8,128)} copy(f32[56,9,128]{2,0,1:T(8,128)S(1)} %bitcast.10) | data formatting | bytes 516096

commit v2 on v1

--- a/solution.py
+++ b/solution.py
@@ -82,6 +82,10 @@
     tr,
     tcat,
     oh,
+    far,
+    flat,
+    g_far,
+    code_far,
     pick,
     nb,
     terms,
@@ -94,6 +98,7 @@
     nb_, nq, ne, nf, nsub, ndom, bp, gp, npd = dims
     rows = 3 * nb_
     nrecv = 3 * nsub * 8
+    rl = round_up(nrecv, 128)
     dom, sub = lax.axis_index("dom"), lax.axis_index("sub")
 
     def peer(direction, k):
@@ -173,6 +178,8 @@
             return carry
 
         lax.fori_loop(1, ORDER, body, 0)
+
+    nt = (((1,), (1,)), ((), ()))
 
     def exchange(phase):
         copies = []
@@ -209,7 +216,6 @@
             ],
             axis=0,
         ).astype(bf16)
-        nt = (((1,), (1,)), ((), ()))
         outgoing = lax.dot_general(
             chosen, tcat[0:npd, :], nt, preferred_element_type=f32
         ) + lax.dot_general(chosen, tcat[npd : 2 * npd, :], nt, preferred_element_type=f32)
@@ -235,26 +241,24 @@
             for p in range(nq):
                 block = source[at, lanes(p)]
                 for q in range(nq):
-                    term = block * matrix[p, q, f : f + 1, :]
+                    term = block * matrix(p, q, f)
                     accs[q] = term if accs[q] is None else accs[q] + term
             for q in range(nq):
                 terms[at, lanes(q)] = accs[q]
 
     def own_side():
-        pick[...] = jnp.dot(tcat[...], oh[0 : nf * ne, :], preferred_element_type=f32)
-        flux(tr, flux_own, True)
-
-    def other_side(phase, copies):
-        for copy in copies:
-            copy.wait()
-        recv[phase, pl.ds(nsub + sub, 1)] = send[phase, pl.ds(nsub + sub, 1)]
-        arrived = recv[phase].reshape(nrecv, npd).T
-        high, low = split_rows(arrived)
-        far = oh[nf * ne : nf * ne + nrecv, :]
-        pick[0:npd, :] = pick[0:npd, :] + jnp.dot(high, far, preferred_element_type=f32)
-        pick[npd : 2 * npd, :] = pick[npd : 2 * npd, :] + jnp.dot(
-            low, far, preferred_element_type=f32
+        pick[...] = jnp.dot(tcat[...], oh[...], preferred_element_type=f32)
+        flux(tr, lambda p, q, f: flux_own[p, q, f : f + 1, :], True)
+
+    def choose(turned, code, at):
+        part = turned[:, at]
+        return jnp.where(
+            code == 0,
+            part[0:gp],
+            jnp.where(code == 1, part[gp : 2 * gp], part[2 * gp : 3 * gp]),
         )
+
+    def near_side():
         r_mat = r_ref[...]
         extra = jnp.zeros((r_mat.shape[1] - 3 * gp, nf * ne), f32)
         for q in range(nq):
@@ -264,19 +268,70 @@
             turned = jnp.dot(r_mat, stacked, preferred_element_type=f32)
             for f in range(nf):
                 code = jnp.broadcast_to(orient[f : f + 1, :], (gp, ne))
-                part = turned[:, lanes(f)]
-                nb[f * gp : (f + 1) * gp, lanes(q)] = jnp.where(
-                    code == 0,
-                    part[0:gp],
-                    jnp.where(code == 1, part[gp : 2 * gp], part[2 * gp : 3 * gp]),
-                )
-        flux(nb, flux_nbr, False)
-        high, low = split_rows(terms[...])
+                nb[f * gp : (f + 1) * gp, lanes(q)] = choose(turned, code, lanes(f))
+        flux(nb, lambda p, q, f: flux_nbr[p, q, f : f + 1, :], False)
+
+    def far_constants():
+        for p in range(nq):
+            for q in range(nq):
+                at = (p * nq + q) * nf
+                flat[at : at + nf, :] = flux_nbr[p, q]
+        total, turn = None, None
+        for f in range(nf):
+            hit = far[0:rl, lanes(f)]
+            high, low = split_rows(flat[pl.ds(f, nq * nq, stride=nf), :])
+            taken = lax.dot_general(high, hit, nt, preferred_element_type=f32)
+            taken = taken + lax.dot_general(low, hit, nt, preferred_element_type=f32)
+            total = taken if total is None else total + taken
+            code = jnp.broadcast_to(orient[f : f + 1, :], (8, ne)).astype(f32).astype(bf16)
+            taken = lax.dot_general(code, hit, nt, preferred_element_type=f32)
+            turn = taken if turn is None else turn + taken
+        g_far[...] = total
+        code_far[...] = turn
+
+    def other_side(phase, copies):
+        for copy in copies:
+            copy.wait()
+        recv[phase, pl.ds(nsub + sub, 1)] = send[phase, pl.ds(nsub + sub, 1)]
+        arrived = recv[phase].reshape(nrecv, npd)
+        if rl > nrecv:
+            arrived = jnp.concatenate([arrived, jnp.zeros((rl - nrecv, npd), f32)], axis=0)
+        arrived = arrived.T
+        r_mat = r_ref[...]
+        wide = jnp.concatenate([arrived[q * gp : (q + 1) * gp] for q in range(nq)], axis=1)
+        high, low = parts(wide)
+        extra = jnp.zeros((r_mat.shape[1] - 3 * gp, nq * rl), f32)
+        stacked = jnp.concatenate([high, high, low, extra], axis=0).astype(bf16)
+        turned = jnp.dot(r_mat, stacked, preferred_element_type=f32)
+        code = jnp.broadcast_to(code_far[0:1, :], (gp, rl))
+        blocks = [choose(turned, code, slice(p * rl, (p + 1) * rl)) for p in range(nq)]
+        sums = []
+        for q in range(nq):
+            total = None
+            for p in range(nq):
+                term = blocks[p] * g_far[p * nq + q : p * nq + q + 1, :]
+                total = term if total is None else total + term
+            sums.append(total)
+        sums.append(jnp.zeros((npd - nq * gp, rl), f32))
+        high, low = split_rows(jnp.concatenate(sums, axis=0))
+        spread = jnp.dot(
+            jnp.concatenate([high, low], axis=1), far[...], preferred_element_type=f32
+        )
         ng = nf * gp
-        tcat3[0:ng, :] = high
-        tcat3[ng : 2 * ng, :] = high
-        tcat3[2 * ng : 3 * ng, :] = low
-        return jnp.dot(l_mat[...], tcat3[...], preferred_element_type=f32)
+        for q in range(nq):
+            whole = jnp.concatenate(
+                [
+                    terms[f * gp : (f + 1) * gp, lanes(q)]
+                    + spread[q * gp : (q + 1) * gp, lanes(f)]
+                    for f in range(nf)
+                ],
+                axis=0,
+            )
+            high, low = split_rows(whole)
+            tcat3[0:ng, lanes(q)] = high
+            tcat3[ng : 2 * ng, lanes(q)] = low
+        both = jnp.dot(l_mat[...], tcat3[...], preferred_element_type=f32)
+        return both[0:nb_] + both[nb_ : 2 * nb_]
 
     def plastic(field, relax, emit):
         s = [field[q][0:1, :] for q in range(6)]
@@ -318,7 +373,9 @@
         for f in range(nf):
             lift_t[f * gp : f * gp + ng, :] = lift[:, f, :]
         high, low = parts(lift_t[...])
-        l_mat[...] = jnp.concatenate([high, low, high], axis=0).T.astype(bf16)
+        first = jnp.concatenate([high, high], axis=0)
+        second = jnp.concatenate([low, jnp.zeros_like(low)], axis=0)
+        l_mat[...] = jnp.concatenate([first.T, second.T], axis=0).astype(bf16)
         rot_s[...] = jnp.zeros_like(rot_s)
         for h in range(3):
             rot_s[h * gp : h * gp + ng, 0:ng] = rotate[h]
@@ -340,15 +397,23 @@
     later_constants()
     for f in range(nf):
         code = face_source[f : f + 1, :]
-        for r in range(0, nf * ne + nrecv, 32):
+        for r in range(0, nf * ne + rl, 32):
             row = lax.broadcasted_iota(jnp.int32, (32, ne), 0) + r
-            oh[r : r + 32, lanes(f)] = jnp.where(row == code, 1.0, 0.0).astype(bf16)
+            hit = jnp.where(row == code, 1.0, 0.0).astype(bf16)
+            if r < nf * ne:
+                oh[r : r + 32, lanes(f)] = hit
+            else:
+                at = r - nf * ne
+                far[at : at + 32, lanes(f)] = hit
+                far[rl + at : rl + at + 32, lanes(f)] = hit
+    far_constants()
 
     def keep(q, x):
         upd[:, lanes(q)] = x
 
     volume(keep)
     own_side()
+    near_side()
     lifted = other_side(0, copies)
     upd[...] = upd[...] - lifted
 
@@ -371,6 +436,7 @@
 
     volume(keep_second)
     own_side()
+    near_side()
     upd[...] = other_side(1, copies)
 
     def write(q, x):
@@ -407,6 +473,7 @@
     npd = round_up(nq * gp, 32)
     rp = round_up(3 * gp, 16)
     nrecv = 3 * nsub * 8
+    rl = round_up(nrecv, 128)
     dims = (nbas, nq, ne, nf, nsub, ndom, bp, gp, npd)
     vmem = pl.BlockSpec(memory_space=pltpu.VMEM)
     wide = nq * ne
@@ -437,7 +504,7 @@
             pltpu.VMEM((3 * gp, gp), f32),
             pltpu.VMEM((3 * nsub, 8), f32),
             pltpu.VMEM((6 * nbas + nf * gp, 3 * bp), bf16),
-            pltpu.VMEM((nbas, 3 * nf * gp), bf16),
+            pltpu.VMEM((2 * nbas, 2 * nf * gp), bf16),
             pltpu.VMEM((3 * gp, rp), bf16),
             pltpu.VMEM((3 * bp, wide), bf16),
             pltpu.VMEM((3 * nbas, wide), f32),
@@ -448,11 +515,15 @@
             pltpu.VMEM((nbas, wide), f32),
             pltpu.VMEM((nf * gp, wide), f32),
             pltpu.VMEM((2 * npd, nf * ne), bf16),
-            pltpu.VMEM((nf * ne + nrecv, nf * ne), bf16),
+            pltpu.VMEM((nf * ne, nf * ne), bf16),
+            pltpu.VMEM((2 * rl, nf * ne), bf16),
+            pltpu.VMEM((nq * nq * nf, ne), f32),
+            pltpu.VMEM((nq * nq, rl), f32),
+            pltpu.VMEM((8, rl), f32),
             pltpu.VMEM((2 * npd, nf * ne), f32),
             pltpu.VMEM((nf * gp, wide), f32),
             pltpu.VMEM((nf * gp, wide), f32),
-            pltpu.VMEM((3 * nf * gp, wide), bf16),
+            pltpu.VMEM((2 * nf * gp, wide), bf16),
             pltpu.VMEM((2, 3 * nsub, 8, npd), f32),
             pltpu.VMEM((2, 3 * nsub, 8, npd), f32),
             pltpu.SemaphoreType.DMA((2, 3 * nsub)),

time: 26 us -> 25.1 us (0.965)
  Pallas kernels: 25.1 us -> 24.2 us
    pallas_call x1, Pallas kernels: 25.1 us -> 24.2 us  [local(): pl.pallas_call(functools.partial(kernel, dims), out_shape=pltpu.VMEM((nq,...]
where the time goes in v2:
time: 25.1 us; the launch traced here: 25 us
  Pallas kernels  24.2 us (96%)
  local copies, waits for them, and re-layouts  0.7 us (3%)
    pallas_call x1, Pallas kernels, local(): pl.pallas_call(functools.partial(kernel, dims), out_shape=pltpu.VMEM((nq,...  24.2 us
    unnamed x1, local copies, waits for them, and re-layouts  0.7 us

profile of v2, /device:TPU:0, one launch (start us, length us, event | category | flops | bytes accessed | tf_op | source)
XLA Modules:
  0.0 25.0 jit_solution(11597918806250898993)
XLA Ops:
  0.0 24.2 %window.1 = f32[9,56,128]{2,1,0:T(8,128)S(1)} custom-call(f32[9,56,128]{2,1,0:T(8,128)} %bitcast.11, f32[9,9,3,128]{3,2,1,0:T(4,128)} %bitcast.12, f32[9,9,4,128]{3,2,1,0:T(4,128)} %bitcast.13, f32[9,9,4,128]{3,2,1,0:T(4,128)} %bitcast.14, f32[1,128]{1,0:T(1,128)} %bitcast.18, s32[1,128]{1,0:T(1,128)} %bitcast.19, s32[4,128]{1,0:T(4,128)} %refs_6_.1, ...), custom_call_target="tpu_custom_call" | custom-call | tf_op jit(solution)/shard_map/window/pallas_call | solution.py:495
  24.3 0.7 %copy.15 = f32[56,9,128]{2,0,1:T(8,128)} copy(f32[56,9,128]{2,0,1:T(8,128)S(1)} %bitcast.10) | data formatting | bytes 516096

commit v3 on v2

--- a/solution.py
+++ b/solution.py
@@ -69,11 +69,13 @@
     lift_t,
     rot_s,
     send_s,
+    chosen_ref,
     a_mat,
     l_mat,
     r_ref,
     cat,
     prod,
+    past,
     u0,
     u1,
     acc1,
@@ -125,7 +127,8 @@
         for n, (source, place) in enumerate(zip(given, loaded))
     ]
     early = (0, 1, 8, 9, 10)
-    for n in list(early) + [n for n in range(len(loads)) if n not in early]:
+    first_loads = (9, 10, 8, 0, 1)
+    for n in list(first_loads) + [n for n in range(len(loads)) if n not in early]:
         loads[n].start()
 
     def lanes(q):
@@ -165,14 +168,18 @@
 
     def series(second_too):
         def body(k, carry):
-            prod[...] = mat_cat(0, rows)
-            w1, w2 = pick_weight(k, 0), pick_weight(k, ORDER)
+            for p in range(0, nq, 2):
+                at = slice(p * ne, min(p + 2, nq) * ne)
+                prod[:, at] = jnp.dot(
+                    a_mat[0:rows, :], cat[:, at], preferred_element_type=f32
+                )
+            w1 = pick_weight(k, 0)
 
             def emit(q, x):
                 put_cat(q, x)
                 acc1[:, lanes(q)] = acc1[:, lanes(q)] + w1 * x
                 if second_too:
-                    acc2[:, lanes(q)] = acc2[:, lanes(q)] + w2 * x
+                    past[k - 1, :, lanes(q)] = x
 
             star_mul(emit)
             return carry
@@ -207,15 +214,7 @@
             high, low = split_rows(jnp.concatenate(own, axis=0))
             tcat[0:npd, lanes(f)] = high
             tcat[npd : 2 * npd, lanes(f)] = low
-        spots = lax.broadcasted_iota(jnp.int32, (8, nf * ne), 1).astype(f32)
-        columns = send_s[...].T
-        chosen = jnp.concatenate(
-            [
-                jnp.where(spots == columns[:, c : c + 1], 1.0, 0.0)
-                for c in range(3 * nsub)
-            ],
-            axis=0,
-        ).astype(bf16)
+        chosen = chosen_ref[...]
         outgoing = lax.dot_general(
             chosen, tcat[0:npd, :], nt, preferred_element_type=f32
         ) + lax.dot_general(chosen, tcat[npd : 2 * npd, :], nt, preferred_element_type=f32)
@@ -354,7 +353,7 @@
     coarse_relax = 1.0 - math.exp(-2.0 * step_time / relax_time)
 
     mats[...] = jnp.zeros_like(mats)
-    for n in early:
+    for n in first_loads[:3]:
         loads[n].wait()
     ng = project.shape[0]
     for d in range(3):
@@ -367,6 +366,15 @@
     a_mat[...] = jnp.concatenate([high, low, high], axis=1).astype(bf16)
     for d in range(3):
         send_s[d * nsub : (d + 1) * nsub, :] = send_rows[d].astype(f32)
+    spots = lax.broadcasted_iota(jnp.int32, (8, nf * ne), 1).astype(f32)
+    columns = send_s[...].T
+    chosen_ref[...] = jnp.concatenate(
+        [
+            jnp.where(spots == columns[:, c : c + 1], 1.0, 0.0)
+            for c in range(3 * nsub)
+        ],
+        axis=0,
+    ).astype(bf16)
 
     def later_constants():
         lift_t[...] = jnp.zeros_like(lift_t)
@@ -383,12 +391,13 @@
         blank = jnp.zeros((r_ref.shape[1] - 3 * gp, 3 * gp), f32)
         r_ref[...] = jnp.concatenate([high, low, high, blank], axis=0).T.astype(bf16)
 
+    loads[0].wait()
     for q in range(nq):
         x = dofs[q]
         u0[:, lanes(q)] = x
         put_cat(q, x)
         acc1[:, lanes(q)] = wts[0] * x
-        acc2[:, lanes(q)] = wts[ORDER] * x
+    loads[1].wait()
     series(True)
     copies = traces(0)
     for n in range(len(loads)):
@@ -411,6 +420,11 @@
     def keep(q, x):
         upd[:, lanes(q)] = x
 
+    for q in range(nq):
+        later = wts[ORDER] * u0[:, lanes(q)]
+        for k in range(1, ORDER):
+            later = later + wts[ORDER + k] * past[k - 1, :, lanes(q)]
+        acc2[:, lanes(q)] = later
     volume(keep)
     own_side()
     near_side()
@@ -503,11 +517,13 @@
             pltpu.VMEM((nf * gp, nbas), f32),
             pltpu.VMEM((3 * gp, gp), f32),
             pltpu.VMEM((3 * nsub, 8), f32),
+            pltpu.VMEM((nrecv, nf * ne), bf16),
             pltpu.VMEM((6 * nbas + nf * gp, 3 * bp), bf16),
             pltpu.VMEM((2 * nbas, 2 * nf * gp), bf16),
             pltpu.VMEM((3 * gp, rp), bf16),
             pltpu.VMEM((3 * bp, wide), bf16),
             pltpu.VMEM((3 * nbas, wide), f32),
+            pltpu.VMEM((ORDER - 1, nbas, wide), f32),
             pltpu.VMEM((nbas, wide), f32),
             pltpu.VMEM((nbas, wide), f32),
             pltpu.VMEM((nbas, wide), f32),

time: 25.1 us -> 24.9 us (level)
  no operation moved by 1% of the time
where the time goes in v3:
time: 24.9 us; the launch traced here: 24.7 us
  Pallas kernels  24 us (96%)
  local copies, waits for them, and re-layouts  0.7 us (3%)
    pallas_call x1, Pallas kernels, local(): pl.pallas_call(functools.partial(kernel, dims), out_shape=pltpu.VMEM((nq,...  24 us
    unnamed x1, local copies, waits for them, and re-layouts  0.7 us

profile of v3, /device:TPU:0, one launch (start us, length us, event | category | flops | bytes accessed | tf_op | source)
XLA Modules:
  0.0 24.7 jit_solution(17963813008712608989)
XLA Ops:
  0.0 24.0 %window.1 = f32[9,56,128]{2,1,0:T(8,128)S(1)} custom-call(f32[9,56,128]{2,1,0:T(8,128)} %bitcast.11, f32[9,9,3,128]{3,2,1,0:T(4,128)} %bitcast.12, f32[9,9,4,128]{3,2,1,0:T(4,128)} %bitcast.13, f32[9,9,4,128]{3,2,1,0:T(4,128)} %bitcast.14, f32[1,128]{1,0:T(1,128)} %bitcast.18, s32[1,128]{1,0:T(1,128)} %bitcast.19, s32[4,128]{1,0:T(4,128)} %refs_6_.1, ...), custom_call_target="tpu_custom_call" | custom-call | tf_op jit(solution)/shard_map/window/pallas_call | solution.py:509
  24.0 0.7 %copy.15 = f32[56,9,128]{2,0,1:T(8,128)} copy(f32[56,9,128]{2,0,1:T(8,128)S(1)} %bitcast.10) | data formatting | bytes 516096
